TPU v7x, 32 devices: a whole 2x2x4 slice. The times are simulated.
32 devices in a mesh: dp: 32 (over z, y, x, core).
Axes of the slice: x: 2, y: 2, z: 4, core: 2. Of those that a mesh axis runs over, the one named last changes fastest.
Arguments:
- tokens: bfloat16 [24576, 1024], P('dp'), may hold values from -6 to 6
- seg_ids: int32 [96, 256], P('dp'), may hold values from 0 to 7, never falling along the last dimension, each value on 1 to 128 neighbouring positions
- w_qkv: bfloat16 [1024, 3072], P('dp'), may hold values from -0.1875 to 0.1875
- w_attn_out: bfloat16 [1024, 1024], P('dp'), may hold values from -1 to 1
- w_in: bfloat16 [1024, 5248], P('dp'), may hold values from -0.1875 to 0.1875
- w_down: bfloat16 [2624, 1024], P(None, 'dp'), may hold values from -0.125 to 0.125
- gain_attn: bfloat16 [1024], P('dp'), may hold values from 0.099609375 to 1.8984375
- gain_mlp: bfloat16 [1024], P('dp'), may hold values from 0.099609375 to 1.8984375
- cotangent: bfloat16 [24576, 1024], P('dp'), may hold values from -6 to 6
Outputs:
- out: bfloat16 [24576, 1024], P('dp')
- tokens_grad: float32 [24576, 1024], P('dp')
- grad_qkv: float32 [1024, 3072], P('dp')
- grad_attn_out: float32 [1024, 1024], P('dp')
- grad_in: float32 [1024, 5248], P('dp')
- grad_down: float32 [2624, 1024], P(None, 'dp')
- grad_gain_attn: float32 [1024], P('dp')
- grad_gain_mlp: float32 [1024], P('dp')
Inputs may be any that keep to these rules, and one draw needn't show every extreme that they name: `seg_ids`: in each micro-batch the numbers never fall along the 256 slots and all 8 numbers occur; each run of equal numbers is one sequence of 1 to 128 tokens, and some run in the draw is exactly 128 long.
All inputs are finite; a program needn't handle non-finite values.
Results may differ from a plain program's by a relative error of at most 0.012.
The roundings to bfloat16 on the way count: a program that leaves them out, or rounds other values in their place, can miss the bound.
Values may be sent and summed in bfloat16 or wider, within the bound.
No kernel may reach another device: no remote copies, remote signals or barrier semaphores. Data moves between devices by JAX's collectives and lax.ppermute only.
A program may use at most 256 MiB of HBM per device.

v0:
```python
import jax
import jax.numpy as jnp
from jax import lax
from jax.sharding import PartitionSpec as P

HEADS = 16
HEAD_DIM = 64
EPSILON = 1e-05
THETA = 160000.0
NEG_BIG = -1e30
ROOT_HALF = 0.7071067811865476
INV_ROOT_TWO_PI = 0.3989422804014327


def positions(seg_row):
    column = lax.broadcasted_iota(jnp.int32, seg_row.shape, seg_row.ndim - 1)
    before = jnp.concatenate(
        [jnp.full(seg_row.shape[:-1] + (1,), -1, jnp.int32), seg_row[..., :-1]], axis=-1
    )
    starts = lax.cummax(jnp.where(seg_row != before, column, 0), axis=seg_row.ndim - 1)
    return column - starts


def rotary_tables(offsets):
    halves = HEAD_DIM // 2
    frequency = jnp.power(
        jnp.float32(THETA), -(jnp.arange(halves, dtype=jnp.float32) * 2.0 / HEAD_DIM)
    )
    angles = offsets.astype(jnp.float32)[:, None] * frequency[None, :]
    angles = jnp.concatenate([angles, angles], axis=-1)
    return (jnp.cos(angles)[:, None, :], jnp.sin(angles)[:, None, :])


def rotate(field):
    halves = field.shape[-1] // 2
    return jnp.concatenate([-field[..., halves:], field[..., :halves]], axis=-1)


def rotate_back(field):
    halves = field.shape[-1] // 2
    return jnp.concatenate([field[..., halves:], -field[..., :halves]], axis=-1)


def gelu_exact(field):
    return 0.5 * field * (1.0 + lax.erf(field * ROOT_HALF))


def gelu_slope(field):
    return (
        0.5 * (1.0 + lax.erf(field * ROOT_HALF))
        + field * jnp.exp(-0.5 * field * field) * INV_ROOT_TWO_PI
    )


def norm_forward(field, gain_row):
    center = field - jnp.mean(field, axis=-1, keepdims=True)
    inv_scale = lax.rsqrt(jnp.mean(center * center, axis=-1, keepdims=True) + EPSILON)
    unit_rows = center * inv_scale
    return (unit_rows * gain_row, unit_rows, inv_scale)


def norm_backward(gradient, unit_rows, inv_scale, gain_row):
    scaled = gradient * gain_row
    inner = (
        scaled
        - jnp.mean(scaled, axis=-1, keepdims=True)
        - unit_rows * jnp.mean(scaled * unit_rows, axis=-1, keepdims=True)
    )
    return (inv_scale * inner, jnp.sum(gradient * unit_rows, axis=0))


def score_block(queries, keys_rot, seg_row):
    scores = jnp.einsum(
        "qhd,khd->hqk", queries, keys_rot, preferred_element_type=jnp.float32
    ) * HEAD_DIM ** (-0.5)
    same_seq = seg_row[:, None] == seg_row[None, :]
    return jnp.where(same_seq[None], scores, NEG_BIG)


def attend(queries, keys_rot, values, seg_row):
    scores = score_block(queries, keys_rot, seg_row)
    row_max = jnp.max(scores, axis=-1, keepdims=True)
    exponent = jnp.exp(scores - row_max)
    row_total = jnp.sum(exponent, axis=-1, keepdims=True)
    probability = (exponent / row_total).astype(jnp.bfloat16)
    attended = jnp.einsum("hqk,khd->qhd", probability, values, preferred_element_type=jnp.float32)
    return (attended.astype(jnp.bfloat16), row_max, row_total)


def attend_backward(queries, keys_rot, values, seg_row, row_max, row_total, grad_att):
    scores = score_block(queries, keys_rot, seg_row)
    probability = jnp.exp(scores - row_max) / row_total
    grad_prob = jnp.einsum("qhd,khd->hqk", grad_att, values, preferred_element_type=jnp.float32)
    grad_values = jnp.einsum(
        "hqk,qhd->khd",
        probability.astype(jnp.bfloat16),
        grad_att,
        preferred_element_type=jnp.float32,
    )
    grad_scores = probability * (
        grad_prob - jnp.sum(grad_prob * probability, axis=-1, keepdims=True)
    )
    grad_scores = grad_scores.astype(jnp.bfloat16)
    grad_queries = jnp.einsum(
        "hqk,khd->qhd", grad_scores, keys_rot, preferred_element_type=jnp.float32
    ) * HEAD_DIM ** (-0.5)
    grad_keys = jnp.einsum(
        "hqk,qhd->khd", grad_scores, queries, preferred_element_type=jnp.float32
    ) * HEAD_DIM ** (-0.5)
    return (grad_queries, grad_keys, grad_values)


def shards(tokens, seg_ids, w_qkv, w_attn_out, w_in, w_down, gain_attn, gain_mlp, cotangent):
    micro_count, block_rows = seg_ids.shape
    model_width = tokens.shape[1]
    hidden_units = w_down.shape[0]

    def weights_now():
        return (
            lax.all_gather(w_qkv, "dp", axis=0, tiled=True),
            lax.all_gather(w_attn_out, "dp", axis=0, tiled=True),
            lax.all_gather(w_in, "dp", axis=0, tiled=True),
            lax.all_gather(w_down, "dp", axis=1, tiled=True),
            lax.all_gather(gain_attn, "dp", axis=0, tiled=True),
            lax.all_gather(gain_mlp, "dp", axis=0, tiled=True),
        )

    stored = []
    outputs = []
    for micro_index in range(micro_count):
        wq_full, wo_full, wi_full, wd_full, ga_full, gm_full = weights_now()
        lower = micro_index * block_rows
        inputs = tokens[lower : lower + block_rows].astype(jnp.float32)
        seg_row = seg_ids[micro_index]
        cosine_table, sine_table = rotary_tables(positions(seg_row))
        normed_attn, unit_attn, inv_attn = norm_forward(inputs, ga_full.astype(jnp.float32))
        normed_attn = normed_attn.astype(jnp.bfloat16)
        projected = jnp.dot(normed_attn, wq_full, preferred_element_type=jnp.float32)
        queries = projected[:, :model_width].reshape(block_rows, HEADS, HEAD_DIM)
        keys_rot = projected[:, model_width : 2 * model_width].reshape(block_rows, HEADS, HEAD_DIM)
        values = (
            projected[:, 2 * model_width :]
            .reshape(block_rows, HEADS, HEAD_DIM)
            .astype(jnp.bfloat16)
        )
        queries = (queries * cosine_table + rotate(queries) * sine_table).astype(jnp.bfloat16)
        keys_rot = (keys_rot * cosine_table + rotate(keys_rot) * sine_table).astype(jnp.bfloat16)
        attended, row_max, row_total = attend(queries, keys_rot, values, seg_row)
        attended = attended.reshape(block_rows, model_width)
        resid = inputs + jnp.dot(attended, wo_full, preferred_element_type=jnp.float32)
        normed_mlp, unit_mlp, inv_mlp = norm_forward(resid, gm_full.astype(jnp.float32))
        normed_mlp = normed_mlp.astype(jnp.bfloat16)
        gate_up = jnp.dot(normed_mlp, wi_full, preferred_element_type=jnp.float32)
        gate = gate_up[:, :hidden_units]
        upward = gate_up[:, hidden_units:]
        activated = gelu_exact(gate)
        hidden = (activated * upward).astype(jnp.bfloat16)
        result = resid + jnp.dot(hidden, wd_full, preferred_element_type=jnp.float32)
        outputs.append(result.astype(jnp.bfloat16))
        stored.append(
            (
                seg_row,
                cosine_table,
                sine_table,
                unit_attn,
                inv_attn,
                normed_attn,
                queries,
                keys_rot,
                values,
                row_max,
                row_total,
                attended,
                unit_mlp,
                inv_mlp,
                normed_mlp,
                gate,
                upward,
                activated,
                hidden,
            )
        )
    summed = None
    input_grads = []
    for micro_index in reversed(range(micro_count)):
        wq_full, wo_full, wi_full, wd_full, ga_full, gm_full = weights_now()
        (
            seg_row,
            cosine_table,
            sine_table,
            unit_attn,
            inv_attn,
            normed_attn,
            queries,
            keys_rot,
            values,
            row_max,
            row_total,
            attended,
            unit_mlp,
            inv_mlp,
            normed_mlp,
            gate,
            upward,
            activated,
            hidden,
        ) = stored[micro_index]
        lower = micro_index * block_rows
        grad_out_b = cotangent[lower : lower + block_rows]
        grad_out = grad_out_b.astype(jnp.float32)
        grad_down = jnp.dot(hidden.T, grad_out_b, preferred_element_type=jnp.float32)
        grad_hidden = jnp.dot(grad_out_b, wd_full.T, preferred_element_type=jnp.float32)
        grad_gate_up = jnp.concatenate(
            [grad_hidden * upward * gelu_slope(gate), grad_hidden * activated], axis=-1
        )
        grad_gate_up = grad_gate_up.astype(jnp.bfloat16)
        grad_in = jnp.dot(normed_mlp.T, grad_gate_up, preferred_element_type=jnp.float32)
        grad_normed_mlp = jnp.dot(grad_gate_up, wi_full.T, preferred_element_type=jnp.float32)
        resid_part, grad_gain_mlp = norm_backward(
            grad_normed_mlp, unit_mlp, inv_mlp, gm_full.astype(jnp.float32)
        )
        grad_resid = grad_out + resid_part
        grad_resid_b = grad_resid.astype(jnp.bfloat16)
        grad_attn = jnp.dot(attended.T, grad_resid_b, preferred_element_type=jnp.float32)
        grad_att = jnp.dot(grad_resid_b, wo_full.T, preferred_element_type=jnp.float32).astype(
            jnp.bfloat16
        )
        grad_att = grad_att.reshape(block_rows, HEADS, HEAD_DIM)
        grad_q_rot, grad_k_rot, grad_values = attend_backward(
            queries, keys_rot, values, seg_row, row_max, row_total, grad_att
        )
        grad_queries = grad_q_rot * cosine_table + rotate_back(grad_q_rot * sine_table)
        grad_keys = grad_k_rot * cosine_table + rotate_back(grad_k_rot * sine_table)
        grad_projected = jnp.concatenate(
            [
                grad_queries.reshape(block_rows, model_width),
                grad_keys.reshape(block_rows, model_width),
                grad_values.reshape(block_rows, model_width),
            ],
            axis=-1,
        ).astype(jnp.bfloat16)
        grad_qkv = jnp.dot(normed_attn.T, grad_projected, preferred_element_type=jnp.float32)
        grad_normed_attn = jnp.dot(grad_projected, wq_full.T, preferred_element_type=jnp.float32)
        input_part, grad_gain_attn = norm_backward(
            grad_normed_attn, unit_attn, inv_attn, ga_full.astype(jnp.float32)
        )
        input_grads.append(grad_resid + input_part)
        grads_now = (grad_qkv, grad_attn, grad_in, grad_down, grad_gain_attn, grad_gain_mlp)
        if summed is None:
            summed = grads_now
        else:
            summed = tuple((earlier + latest for earlier, latest in zip(summed, grads_now)))
    summed = (
        lax.psum_scatter(summed[0], "dp", scatter_dimension=0, tiled=True),
        lax.psum_scatter(summed[1], "dp", scatter_dimension=0, tiled=True),
        lax.psum_scatter(summed[2], "dp", scatter_dimension=0, tiled=True),
        lax.psum_scatter(summed[3], "dp", scatter_dimension=1, tiled=True),
        lax.psum_scatter(summed[4], "dp", scatter_dimension=0, tiled=True),
        lax.psum_scatter(summed[5], "dp", scatter_dimension=0, tiled=True),
    )
    return (
        jnp.concatenate(outputs, axis=0),
        jnp.concatenate(input_grads[::-1], axis=0),
        summed[0],
        summed[1],
        summed[2],
        summed[3],
        summed[4],
        summed[5],
    )


def solution(mesh):
    return jax.shard_map(
        shards,
        mesh=mesh,
        in_specs=(
            P("dp", None),
            P("dp", None),
            P("dp", None),
            P("dp", None),
            P("dp", None),
            P(None, "dp"),
            P("dp"),
            P("dp"),
            P("dp", None),
        ),
        out_specs=(
            P("dp", None),
            P("dp", None),
            P("dp", None),
            P("dp", None),
            P("dp", None),
            P(None, "dp"),
            P("dp"),
            P("dp"),
        ),
        check_vma=False,
    )
```

profile of v0, /device:TPU:14, one launch (start us, length us, event | category | flops | bytes accessed | tf_op | source)
XLA Modules:
  0.0 1046.7 jit_solution(11209581067904707399)
XLA Ops:
  14.5 41.1 %all-reduce.5 = (bf16[1024]{0:T(1024)(128)(2,1)S(1)}, bf16[1024]{0:T(1024)(128)(2,1)S(1)}) all-reduce(bf16[1024]{0:T(1024)(128)(2,1)S(1)} %dynamic-update-slice, bf16[1024]{0:T(1024)(128)(2,1)S(1)} %dynamic-update-slice.1), channel_id=1, replica_groups=mesh['dp'=32] {'dp'}, use_global_device_ids=true, to_apply=%add | all-reduce | flops 2048 | bytes 8192
  62.3 18.4 %all-gather.5.cloned.1.call-done = bf16[1024,3072]{1,0:T(8,128)(2,1)} async-done(((bf16[32,3072]{1,0:T(8,128)(2,1)}), bf16[1024,3072]{1,0:T(8,128)(2,1)}) %all-gather.5.cloned.1.call-update) | async-done | bytes 6291472 | tf_op jit(solution)/shard_map/all_gather | solution.py:120
  128.4 9.3 all-gather.7.cloned.1.call-done
  164.9 62.8 %all-gather.9.cloned.1.call-done = bf16[1024,5248]{1,0:T(8,128)(2,1)} async-done(((bf16[32,5248]{1,0:T(8,128)(2,1)}), bf16[1024,5248]{1,0:T(8,128)(2,1)}) %all-gather.9.cloned.1.call-update) | async-done | bytes 10747920 | tf_op jit(solution)/shard_map/all_gather | solution.py:122
  227.7 9.1 fusion.175
  241.8 53.9 %all-gather.11.cloned.1.call-done = bf16[2624,1024]{0,1:T(8,128)(2,1)} async-done(((bf16[2624,32]{0,1:T(8,128)(2,1)}), bf16[2624,1024]{0,1:T(8,128)(2,1)}) %all-gather.11.cloned.1.call-update) | async-done | bytes 5373968 | tf_op jit(solution)/shard_map/all_gather | solution.py:123
  295.8 7.9 fusion.23
  303.7 7.1 fusion.17
  314.9 7.5 multiply_reduce_fusion.4
  326.9 9.5 fusion.11
  336.4 11.5 %multiply_add_fusion.1 = (f32[256,1024]{1,0:T(8,128)S(1)}, f32[256,1024]{1,0:T(8,128)}, f32[256]{0:T(256)S(1)}, f32[256]{0:T(256)S(1)}, f32[1024]{0:T(1024)}, /*index=5*/f32[256,1024]{1,0:T(8,128)}) fusion(f32[256,1024]{1,0:T(8,128)} %get-tuple-element.139, f32[256,1024]{1,0:T(8,128)S(1)} %copy-done.13, f32[256]{0:T(256)S(1)} %broadcast_multiply_fusion.21, ...), kind=kOutput, calls=%fused_computation.187 | convolution fusion | flops 2763651584 | bytes 22892544 | tf_op jit(solution)/shard_map/dot_general | solution.py:218
  359.3 6.8 fusion.113
  366.1 12.3 %add_add_fusion.2 = f32[2624,1024]{0,1:T(8,128)} fusion(f32[2624,1024]{0,1:T(8,128)S(1)} %fusion.109, f32[2624,1024]{0,1:T(8,128)} %fusion.113, bf16[768,1024]{1,0:T(8,128)(2,1)} %param.17, f32[256,5248]{1,0:T(8,128)} %copy-done.18), kind=kOutput, calls=%fused_computation.5 | convolution fusion | flops 1385136128 | bytes 38535168 | tf_op jit(solution)/shard_map/dot_general | solution.py:211
  414.4 6.6 fusion.104
  421.8 6.6 fusion.106
  429.2 13.8 %add_add_fusion.1 = f32[1024,3072]{1,0:T(8,128)} fusion(f32[1024,3072]{1,0:T(8,128)} %fusion.104, f32[1024,3072]{1,0:T(8,128)} %fusion.106, bf16[256,1024]{0,1:T(8,128)(2,1)S(1)} %bitcast.185, bf16[256,1024]{0,1:T(8,128)(2,1)S(1)} %bitcast.169, bf16[256,1024]{0,1:T(8,128)(2,1)S(1)} %bitcast.167, f32[1024]{0:T(1024)S(1)} %copy-done.71, ...), kind=kOutput, calls=%fused_computation.4 | convolution fusion | flops 1622933504 | bytes 39852032 | tf_op jit(solution)/shard_map/dot_general | solution.py:242
  444.3 11.0 %fusion.33 = f32[1024,5248]{1,0:T(8,128)} fusion(bf16[256,2624]{1,0:T(8,128)(2,1)} %copy-done.59, bf16[256,2624]{1,0:T(8,128)(2,1)} %copy-done.58, f32[256,1024]{1,0:T(8,128)S(1)} %copy-done.10, f32[256]{0:T(256)S(1)} %add_rsqrt_fusion, f32[256]{0:T(256)S(1)} %broadcast_multiply_fusion.27, f32[1024]{0:T(1024)S(1)} %convert_element_type.194), kind=kOutput, calls=%fused_computation.71 | convolution fusion | flops 2757885952 | bytes 25237504 | tf_op jit(solution)/shard_map/dot_general | solution.py:217
  455.4 9.2 fusion.35
  464.6 23.6 %add_add_fusion = f32[1024,5248]{1,0:T(8,128)} fusion(f32[1024,5248]{1,0:T(8,128)} %fusion.33, f32[1024,5248]{1,0:T(8,128)} %fusion.35, bf16[256,2624]{1,0:T(8,128)(2,1)S(1)} %copy-done.63, bf16[256,2624]{1,0:T(8,128)(2,1)S(1)} %copy-done.62, f32[256,1024]{1,0:T(8,128)S(1)} %copy-done.6, f32[1024]{0:T(1024)S(1)} %convert_element_type.194, ...), kind=kOutput, calls=%fused_computation.3 | convolution fusion | flops 2768633856 | bytes 68229120 | tf_op jit(solution)/shard_map/dot_general | solution.py:217
  488.2 5.2 fusion.107
  502.4 40.0 %all-reduce.4 = (f32[1024]{0:T(1024)S(1)}, f32[1024]{0:T(1024)S(1)}) all-reduce(f32[1024]{0:T(1024)S(1)} %add_add_fusion.5, f32[1024]{0:T(1024)S(1)} %add_add_fusion.4), channel_id=6, replica_groups=mesh['dp'=32] {'dp'}, use_global_device_ids=true, to_apply=%region_46.47.clone | all-reduce | flops 2048 | bytes 16384
  561.3 80.5 %reduce-scatter.11.cloned.1.call-done = f32[2624,32]{0,1:T(8,128)} async-done(((f32[2624,1024]{0,1:T(8,128)}), f32[2624,32]{0,1:T(8,128)}) %reduce-scatter.11.cloned.1.call-update) | async-done | bytes 335888 | tf_op jit(solution)/shard_map/reduce_scatter | solution.py:257
  641.7 161.3 %reduce-scatter.5.cloned.1.call-done = f32[32,3072]{1,0:T(8,128)} async-done(((f32[1024,3072]{1,0:T(8,128)}), f32[32,3072]{1,0:T(8,128)}) %reduce-scatter.5.cloned.1.call-update) | async-done | bytes 393232 | tf_op jit(solution)/shard_map/reduce_scatter | solution.py:254
  803.1 236.6 %reduce-scatter.9.cloned.1.call-done = f32[32,5248]{1,0:T(8,128)} async-done(((f32[1024,5248]{1,0:T(8,128)}), f32[32,5248]{1,0:T(8,128)}) %reduce-scatter.9.cloned.1.call-update) | async-done | bytes 671760 | tf_op jit(solution)/shard_map/reduce_scatter | solution.py:256
  (419 shorter events, 179.1 us)
Async XLA Ops:
  7.2 73.5 %all-gather.5.cloned.1.call-start = ((), (), s32[]{:S(2)}) async-start(), calls=%async_computation.4 | async-start | bytes 6488064 | tf_op jit(solution)/shard_map/all_gather | solution.py:120
  7.9 129.8 %all-gather.7.cloned.1.call-start = ((), (), s32[]{:S(2)}) async-start(), calls=%async_computation.5 | async-start | bytes 2162688 | tf_op jit(solution)/shard_map/all_gather | solution.py:121
  8.7 219.0 %all-gather.9.cloned.1.call-start = ((), (), s32[]{:S(2)}) async-start(), calls=%async_computation.6 | async-start | bytes 11083776 | tf_op jit(solution)/shard_map/all_gather | solution.py:122
  9.4 286.3 %all-gather.11.cloned.1.call-start = ((), (), s32[]{:S(2)}) async-start(), calls=%async_computation.7 | async-start | bytes 5677056 | tf_op jit(solution)/shard_map/all_gather | solution.py:123
  10.0 551.3 %reduce-scatter.7.cloned.1.call-start = ((), (), s32[]{:S(2)}) async-start(), calls=%async_computation.9 | async-start | bytes 4325376 | tf_op jit(solution)/shard_map/reduce_scatter | solution.py:255
  13.3 88.7 %copy-start.105 = (f32[256]{0:T(256)}, f32[256]{0:T(256)S(1)}, u32[]{:S(2)}) copy-start(f32[256]{0:T(256)S(1)} %broadcast_multiply_fusion.32) | copy-start | bytes 3076
  13.3 72.2 %copy-start.97 = (f32[256]{0:T(256)}, f32[256]{0:T(256)S(1)}, u32[]{:S(2)}) copy-start(f32[256]{0:T(256)S(1)} %get-tuple-element.151) | copy-start | bytes 3076
  13.3 74.1 %copy-start.95 = (f32[256]{0:T(256)}, f32[256]{0:T(256)S(1)}, u32[]{:S(2)}) copy-start(f32[256]{0:T(256)S(1)} %get-tuple-element.152) | copy-start | bytes 3076
  13.9 71.6 %copy-start.101 = (f32[256]{0:T(256)}, f32[256]{0:T(256)S(1)}, u32[]{:S(2)}) copy-start(f32[256]{0:T(256)S(1)} %add_rsqrt_fusion.1) | copy-start | bytes 3076
  55.6 46.4 %copy-start.70 = (f32[1024]{0:T(1024)}, f32[1024]{0:T(1024)S(1)}, u32[]{:S(2)}) copy-start(f32[1024]{0:T(1024)S(1)} %convert_element_type.185) | copy-start | bytes 12292
  59.3 28.2 %copy-start.99 = (f32[256]{0:T(256)}, f32[256]{0:T(256)S(1)}, u32[]{:S(2)}) copy-start(f32[256]{0:T(256)S(1)} %add_rsqrt_fusion.3) | copy-start | bytes 3076
  60.8 41.3 %copy-start.107 = (f32[256]{0:T(256)}, f32[256]{0:T(256)S(1)}, u32[]{:S(2)}) copy-start(f32[256]{0:T(256)S(1)} %add_rsqrt_fusion.5) | copy-start | bytes 3076
  128.4 13.4 %copy-start.43 = (bf16[16,64,256]{2,1,0:T(8,128)(2,1)}, bf16[16,64,256]{2,1,0:T(8,128)(2,1)S(1)}, u32[]{:S(2)}) copy-start(bf16[16,64,256]{2,1,0:T(8,128)(2,1)S(1)} %convolution_convert_fusion.6) | copy-start | bytes 1572868
  161.5 66.2 %copy-start.8 = (f32[256,1024]{1,0:T(8,128)S(1)}, f32[256,1024]{1,0:T(8,128)}, u32[]{:S(2)}) copy-start(f32[256,1024]{1,0:T(8,128)} %copy-done.7) | copy-start | bytes 3145732
  295.8 15.0 %slice-start = ((s8[10747904]{0:T(1024)(128)(4,1)}), s8[4194304]{0:T(1024)(128)(4,1)S(1)}, s32[]{:S(2)}) async-start(s8[10747904]{0:T(1024)(128)(4,1)} %bitcast.151), calls=%async_computation.12 | async-start | bytes 8388608
  295.8 15.0 %slice-start.1 = ((s8[10747904]{0:T(1024)(128)(4,1)}), s8[4194304]{0:T(1024)(128)(4,1)S(1)}, s32[]{:S(2)}) async-start(s8[10747904]{0:T(1024)(128)(4,1)} %bitcast.151), calls=%async_computation.13 | async-start | bytes 8388608
  353.2 35.2 %copy-start.16 = (f32[256,1024]{1,0:T(8,128)}, f32[256,1024]{1,0:T(8,128)S(1)}, u32[]{:S(2)}) copy-start(f32[256,1024]{1,0:T(8,128)S(1)} %multiply_add_fusion.2) | copy-start | bytes 3145732
  355.9 285.8 %reduce-scatter.11.cloned.1.call-start = ((), (), s32[]{:S(2)}) async-start(), calls=%async_computation.11 | async-start | bytes 11354112 | tf_op jit(solution)/shard_map/reduce_scatter | solution.py:257
  378.3 424.7 %reduce-scatter.5.cloned.1.call-start = ((), (), s32[]{:S(2)}) async-start(), calls=%async_computation.8 | async-start | bytes 12976128 | tf_op jit(solution)/shard_map/reduce_scatter | solution.py:254
  391.1 12.7 %copy-start.79 = (bf16[256,1024]{0,1:T(8,128)(2,1)}, bf16[256,1024]{0,1:T(8,128)(2,1)S(1)}, u32[]{:S(2)}) copy-start(bf16[256,1024]{0,1:T(8,128)(2,1)S(1)} %copy.109) | copy-start | bytes 1572868
  412.8 16.4 %copy-start.33 = (bf16[256,16,64]{0,2,1:T(8,128)(2,1)}, bf16[256,16,64]{0,2,1:T(8,128)(2,1)S(1)}, u32[]{:S(2)}) copy-start(bf16[256,16,64]{0,2,1:T(8,128)(2,1)S(1)} %get-tuple-element.93) | copy-start | bytes 1572868
  429.2 13.9 %copy-start.72 = (bf16[16,64,256]{2,1,0:T(8,128)(2,1)}, bf16[16,64,256]{2,1,0:T(8,128)(2,1)S(1)}, u32[]{:S(2)}) copy-start(bf16[16,64,256]{2,1,0:T(8,128)(2,1)S(1)} %convolution_convert_fusion.4) | copy-start | bytes 1572868
  443.1 596.6 %reduce-scatter.9.cloned.1.call-start = ((), (), s32[]{:S(2)}) async-start(), calls=%async_computation.10 | async-start | bytes 22167552 | tf_op jit(solution)/shard_map/reduce_scatter | solution.py:256
  444.3 11.0 %copy-start.61 = (bf16[256,2624]{1,0:T(8,128)(2,1)S(1)}, bf16[256,2624]{1,0:T(8,128)(2,1)}, u32[]{:S(2)}) copy-start(bf16[256,2624]{1,0:T(8,128)(2,1)} %get-tuple-element.41) | copy-start | bytes 4030468
  (109 other events, 458.8 us)
Sparse Core Ops, SparseCore 0:
  10.9 69.7 all-gather.4
  83.5 54.2 all-gather.6
  140.6 87.0 all-gather.8
  230.4 65.2 all-gather.10
  356.1 107.6 reduce-scatter.6
  470.2 171.4 reduce-scatter.10
  648.3 154.6 reduce-scatter.4
  806.0 233.5 reduce-scatter.8
where the time goes:
time: 1050 us
  waiting for transfers between devices  625 us (60%)
  matrix products  249 us (24%)
  blocking collectives  81.2 us (8%)
  local copies, waits for them, and re-layouts  49.3 us (5%)
  other arithmetic  24.8 us (2%)
  between operations  16 us (2%)
    reduce_scatter x1, waiting for transfers between devices, shards(): lax.psum_scatter(summed[2], 'dp', scatter_dimension=0, tiled=True)  237 us
    reduce_scatter x1, waiting for transfers between devices, shards(): lax.psum_scatter(summed[0], 'dp', scatter_dimension=0, tiled=True)  161 us
    unnamed x2, blocking collectives  81.2 us
    reduce_scatter x1, waiting for transfers between devices, shards(): lax.psum_scatter(summed[3], 'dp', scatter_dimension=1, tiled=True)  80.5 us
    all_gather x1, waiting for transfers between devices, weights_now(): lax.all_gather(w_in, 'dp', axis=0, tiled=True)  62.8 us
    all_gather x1, waiting for transfers between devices, weights_now(): lax.all_gather(w_down, 'dp', axis=1, tiled=True)  53.9 us
    dot_general x3, matrix products, shards(): jnp.dot(normed_mlp.T, grad_gate_up, preferred_element_type=jnp.float32)  43.8 us
    dot_general x3, matrix products, shards(): jnp.dot(normed_attn.T, grad_projected, preferred_element_type=jnp.float32)  27 us
  transfers between devices with their start and end apart: 8, of which 7 were waited for; matrix products, arithmetic and copies ran while one was open for 24% of the time, Pallas kernels for 0%

commit v1 on v0

--- a/solution.py
+++ b/solution.py
@@ -10,6 +10,22 @@
 NEG_BIG = -1e30
 ROOT_HALF = 0.7071067811865476
 INV_ROOT_TWO_PI = 0.3989422804014327
+
+
+def raise_hubs(comm_axis, x_in):
+    t1 = lax.axis_index(comm_axis)
+    a_now = lax.axis_size(comm_axis)
+    current_block, b_now, val2 = (a_now, t1, x_in.shape[0])
+    value_now, side_arr = (x_in, 1)
+    while side_arr < current_block:
+        new = lax.ppermute(
+            value_now,
+            comm_axis,
+            [(pp, (pp - side_arr) % current_block) for pp in range(current_block)],
+        )
+        value_now = jnp.concatenate([value_now, new], axis=0)
+        side_arr = 2 * side_arr
+    return jnp.roll(value_now, shift=b_now * val2, axis=0)
 
 
 def positions(seg_row):
@@ -119,7 +135,7 @@
         return (
             lax.all_gather(w_qkv, "dp", axis=0, tiled=True),
             lax.all_gather(w_attn_out, "dp", axis=0, tiled=True),
-            lax.all_gather(w_in, "dp", axis=0, tiled=True),
+            raise_hubs("dp", w_in),
             lax.all_gather(w_down, "dp", axis=1, tiled=True),
             lax.all_gather(gain_attn, "dp", axis=0, tiled=True),
             lax.all_gather(gain_mlp, "dp", axis=0, tiled=True),

time: 1050 us -> 1290 us (1.23)
  blocking collectives: 81.2 us -> 295 us
  other arithmetic: 24.8 us -> 40.1 us
  local copies, waits for them, and re-layouts: 49.3 us -> 62.6 us
    unnamed x2, blocking collectives: 81.2 us -> 295 us
    ppermute x0 -> x5, waiting for transfers between devices: none -> 138 us  [raise_hubs(): lax.ppermute(value_now, comm_axis, [(pp, (pp - side_arr) % current_block)...]
    all_gather x1 -> x0, waiting for transfers between devices: 62.8 us -> none  [weights_now(): lax.all_gather(w_in, 'dp', axis=0, tiled=True)]
    all_gather x1, waiting for transfers between devices: 53.9 us -> 0.02 us  [weights_now(): lax.all_gather(w_down, 'dp', axis=1, tiled=True)]
    all_gather x1, waiting for transfers between devices: 18.4 us -> 0.02 us  [weights_now(): lax.all_gather(w_qkv, 'dp', axis=0, tiled=True)]
    concatenate x0 -> x4, other arithmetic: none -> 15.8 us  [the longest x1 12.4 us: raise_hubs(): return jnp.roll(value_now, shift=b_now * val2, axis=0)]
  transfers between devices with their start and end apart: 8 -> 12, of which waited for: 7 -> 7; matrix products, arithmetic and copies ran while one was open for 24% -> 22% of each run, Pallas kernels for 0% -> 0%
where the time goes in v1:
time: 1290 us
  waiting for transfers between devices  614 us (48%)
  blocking collectives  295 us (23%)
  matrix products  252 us (20%)
  local copies, waits for them, and re-layouts  62.6 us (5%)
  other arithmetic  40.1 us (3%)
  between operations  16.3 us (1%)
    unnamed x2, blocking collectives  295 us
    reduce_scatter x1, waiting for transfers between devices, shards(): lax.psum_scatter(summed[2], 'dp', scatter_dimension=0, tiled=True)  237 us
    reduce_scatter x1, waiting for transfers between devices, shards(): lax.psum_scatter(summed[0], 'dp', scatter_dimension=0, tiled=True)  161 us
    ppermute x5, waiting for transfers between devices, raise_hubs(): lax.ppermute(value_now, comm_axis, [(pp, (pp - side_arr) % current_block)...  138 us
    reduce_scatter x1, waiting for transfers between devices, shards(): lax.psum_scatter(summed[3], 'dp', scatter_dimension=1, tiled=True)  77.4 us
    dot_general x3, matrix products, shards(): jnp.dot(normed_mlp.T, grad_gate_up, preferred_element_type=jnp.float32)  45.2 us
    dot_general x3, matrix products, shards(): jnp.dot(grad_gate_up, wi_full.T, preferred_element_type=jnp.float32)  27.3 us
    dot_general x3, matrix products, shards(): jnp.dot(normed_attn.T, grad_projected, preferred_element_type=jnp.float32)  26.8 us
  transfers between devices with their start and end apart: 12, of which 7 were waited for; matrix products, arithmetic and copies ran while one was open for 22% of the time, Pallas kernels for 0%

profile of v1, /device:TPU:14, one launch (start us, length us, event | category | flops | bytes accessed | tf_op | source)
XLA Modules:
  0.0 1287.1 jit_solution(4832170331065162172)
XLA Ops:
  15.5 20.0 %collective-permute-done.1 = bf16[64,5248]{1,0:T(8,128)(2,1)S(1)} collective-permute-done((bf16[64,5248]{1,0:T(8,128)(2,1)S(1)}, bf16[64,5248]{1,0:T(8,128)(2,1)S(1)}, u32[]{:S(2)}, u32[]{:S(2)}) %collective-permute-start.1) | collective-permute-done | bytes 671776 | tf_op jit(solution)/shard_map/ppermute | solution.py:21
  37.7 40.4 %collective-permute-done.2 = bf16[128,5248]{1,0:T(8,128)(2,1)S(1)} collective-permute-done((bf16[128,5248]{1,0:T(8,128)(2,1)}, bf16[128,5248]{1,0:T(8,128)(2,1)S(1)}, u32[]{:S(2)}, u32[]{:S(2)}) %collective-permute-start.2) | collective-permute-done | bytes 1343520 | tf_op jit(solution)/shard_map/ppermute | solution.py:21
  83.5 72.7 %collective-permute-done.3 = bf16[256,5248]{1,0:T(8,128)(2,1)S(1)} collective-permute-done((bf16[256,5248]{1,0:T(8,128)(2,1)S(1)}, bf16[256,5248]{1,0:T(8,128)(2,1)S(1)}, u32[]{:S(2)}, u32[]{:S(2)}) %collective-permute-start.3) | collective-permute-done | bytes 2687008 | tf_op jit(solution)/shard_map/ppermute | solution.py:21
  164.1 252.4 %all-reduce.5 = (bf16[1024]{0:T(1024)(128)(2,1)S(1)}, bf16[1024]{0:T(1024)(128)(2,1)S(1)}) all-reduce(bf16[1024]{0:T(1024)(128)(2,1)S(1)} %dynamic-update-slice, bf16[1024]{0:T(1024)(128)(2,1)S(1)} %dynamic-update-slice.1), channel_id=1, replica_groups=mesh['dp'=32] {'dp'}, use_global_device_ids=true, to_apply=%add | all-reduce | flops 2048 | bytes 8192
  429.4 12.4 fusion.3
  534.1 7.7 fusion.24
  541.9 9.2 fusion.35
  551.1 8.8 fusion.18
  559.9 7.2 multiply_reduce_fusion.4
  567.1 8.4 fusion.12
  575.6 11.0 multiply_add_fusion.1
  597.1 5.7 fusion.114
  602.8 12.0 add_add_fusion.2
  653.4 6.5 fusion.105
  660.8 6.6 fusion.107
  669.0 13.7 %add_add_fusion.1 = f32[1024,3072]{1,0:T(8,128)} fusion(f32[1024,3072]{1,0:T(8,128)} %fusion.105, f32[1024,3072]{1,0:T(8,128)} %fusion.107, bf16[256,1024]{0,1:T(8,128)(2,1)S(1)} %bitcast.187, bf16[256,1024]{0,1:T(8,128)(2,1)S(1)} %bitcast.171, bf16[256,1024]{0,1:T(8,128)(2,1)S(1)} %bitcast.169, f32[1024]{0:T(1024)S(1)} %copy-done.69, ...), kind=kOutput, calls=%fused_computation.6 | convolution fusion | flops 1622933504 | bytes 39852032 | tf_op jit(solution)/shard_map/dot_general | solution.py:258
  682.9 12.7 fusion.34
  695.5 9.4 fusion.36
  705.0 23.1 %add_add_fusion = f32[1024,5248]{1,0:T(8,128)} fusion(f32[1024,5248]{1,0:T(8,128)} %fusion.34, f32[1024,5248]{1,0:T(8,128)} %fusion.36, bf16[256,2624]{1,0:T(8,128)(2,1)S(1)} %copy-done.61, bf16[256,2624]{1,0:T(8,128)(2,1)S(1)} %copy-done.60, f32[256,1024]{1,0:T(8,128)S(1)} %get-tuple-element.149, f32[1024]{0:T(1024)S(1)} %convert_element_type.194, ...), kind=kOutput, calls=%fused_computation.5 | convolution fusion | flops 2768633856 | bytes 68229120 | tf_op jit(solution)/shard_map/dot_general | solution.py:233
  742.4 42.8 %all-reduce.4 = (f32[1024]{0:T(1024)S(1)}, f32[1024]{0:T(1024)S(1)}) all-reduce(f32[1024]{0:T(1024)S(1)} %add_add_fusion.5, f32[1024]{0:T(1024)S(1)} %add_add_fusion.4), channel_id=6, replica_groups=mesh['dp'=32] {'dp'}, use_global_device_ids=true, to_apply=%region_46.48.clone | all-reduce | flops 2048 | bytes 16384
  791.5 5.5 fusion.40
  804.9 77.4 %reduce-scatter.11.cloned.1.call-done = f32[2624,32]{0,1:T(8,128)} async-done(((f32[2624,1024]{0,1:T(8,128)}), f32[2624,32]{0,1:T(8,128)}) %reduce-scatter.11.cloned.1.call-update) | async-done | bytes 335888 | tf_op jit(solution)/shard_map/reduce_scatter | solution.py:273
  882.3 160.8 %reduce-scatter.5.cloned.1.call-done = f32[32,3072]{1,0:T(8,128)} async-done(((f32[1024,3072]{1,0:T(8,128)}), f32[32,3072]{1,0:T(8,128)}) %reduce-scatter.5.cloned.1.call-update) | async-done | bytes 393232 | tf_op jit(solution)/shard_map/reduce_scatter | solution.py:270
  1043.2 236.6 %reduce-scatter.9.cloned.1.call-done = f32[32,5248]{1,0:T(8,128)} async-done(((f32[1024,5248]{1,0:T(8,128)}), f32[32,5248]{1,0:T(8,128)}) %reduce-scatter.9.cloned.1.call-update) | async-done | bytes 671760 | tf_op jit(solution)/shard_map/reduce_scatter | solution.py:272
  (444 shorter events, 207.5 us)
Async XLA Ops:
  7.2 71.0 %copy-start.23 = (bf16[32,5248]{1,0:T(8,128)(2,1)S(1)}, bf16[32,5248]{1,0:T(8,128)(2,1)}, u32[]{:S(2)}) copy-start(bf16[32,5248]{1,0:T(8,128)(2,1)} %param.15) | copy-start | bytes 1007620
  7.2 434.6 %all-gather.4.cloned.1.call-start = ((), (), s32[]{:S(2)}) async-start(), calls=%async_computation.4 | async-start | bytes 6488064 | tf_op jit(solution)/shard_map/all_gather | solution.py:136
  7.9 483.2 %all-gather.6.cloned.1.call-start = ((), (), s32[]{:S(2)}) async-start(), calls=%async_computation.5 | async-start | bytes 2162688 | tf_op jit(solution)/shard_map/all_gather | solution.py:137
  8.0 5.1 collective-permute-start
  14.0 21.5 %collective-permute-start.1 = (bf16[64,5248]{1,0:T(8,128)(2,1)S(1)}, bf16[64,5248]{1,0:T(8,128)(2,1)S(1)}, u32[]{:S(2)}, u32[]{:S(2)}) collective-permute-start(bf16[64,5248]{1,0:T(8,128)(2,1)S(1)} %pad_maximum_fusion.16), channel_id=1, source_target_pairs={{0,30},{1,31},{2,0},{3,1},{4,2},{5,3},{6,4},{7,5},{8,6},{9,7},{10,... | collective-permute-start | bytes 2015240 | tf_op jit(solution)/shard_map/ppermute | solution.py:21
  37.7 40.5 %collective-permute-start.2 = (bf16[128,5248]{1,0:T(8,128)(2,1)}, bf16[128,5248]{1,0:T(8,128)(2,1)S(1)}, u32[]{:S(2)}, u32[]{:S(2)}) collective-permute-start(bf16[128,5248]{1,0:T(8,128)(2,1)} %pad_maximum_fusion.15), channel_id=1, source_target_pairs={{0,28},{1,29},{2,30},{3,31},{4,0},{5,1},{6,2},{7,3},{8,4},{9,5},{1... | collective-permute-start | bytes 4030472 | tf_op jit(solution)/shard_map/ppermute | solution.py:21
  37.7 496.4 %all-gather.8.cloned.1.call-start = ((), (), s32[]{:S(2)}) async-start(), calls=%async_computation.6 | async-start | bytes 5677056 | tf_op jit(solution)/shard_map/all_gather | solution.py:139
  78.4 77.8 %collective-permute-start.3 = (bf16[256,5248]{1,0:T(8,128)(2,1)S(1)}, bf16[256,5248]{1,0:T(8,128)(2,1)S(1)}, u32[]{:S(2)}, u32[]{:S(2)}) collective-permute-start(bf16[256,5248]{1,0:T(8,128)(2,1)S(1)} %pad_maximum_fusion.1), channel_id=1, source_target_pairs={{0,24},{1,25},{2,26},{3,27},{4,28},{5,29},{6,30},{7,31},{8,0},{9,1... | collective-permute-start | bytes 8060936 | tf_op jit(solution)/shard_map/ppermute | solution.py:21
  156.2 260.3 %copy-start.106 = (s32[3,256]{1,0:T(4,128)S(1)}, s32[3,256]{1,0:T(4,128)}, u32[]{:S(2)}) copy-start(s32[3,256]{1,0:T(4,128)} %param.12) | copy-start | bytes 9220
  156.2 264.8 %copy-start.3 = (bf16[768,1024]{1,0:T(8,128)(2,1)S(1)}, bf16[768,1024]{1,0:T(8,128)(2,1)}, u32[]{:S(2)}) copy-start(bf16[768,1024]{1,0:T(8,128)(2,1)} %param.11) | copy-start | bytes 4718596
  158.9 265.2 %collective-permute-start.4 = (bf16[512,5248]{1,0:T(8,128)(2,1)}, bf16[512,5248]{1,0:T(8,128)(2,1)}, u32[]{:S(2)}, u32[]{:S(2)}) collective-permute-start(bf16[512,5248]{1,0:T(8,128)(2,1)} %get-tuple-element.55), channel_id=1, source_target_pairs={{0,16},{1,17},{2,18},{3,19},{4,20},{5,21},{6,22},{7,23},{8,24},{9,... | collective-permute-start | bytes 16121864 | tf_op jit(solution)/shard_map/ppermute | solution.py:21
  163.6 641.3 %reduce-scatter.7.cloned.1.call-start = ((), (), s32[]{:S(2)}) async-start(), calls=%async_computation.8 | async-start | bytes 4325376 | tf_op jit(solution)/shard_map/reduce_scatter | solution.py:271
  416.5 47.3 %copy-start.68 = (f32[1024]{0:T(1024)}, f32[1024]{0:T(1024)S(1)}, u32[]{:S(2)}) copy-start(f32[1024]{0:T(1024)S(1)} %convert_element_type.185) | copy-start | bytes 12292
  421.3 42.5 %copy-start.104 = (f32[256]{0:T(256)}, f32[256]{0:T(256)S(1)}, u32[]{:S(2)}) copy-start(f32[256]{0:T(256)S(1)} %broadcast_multiply_fusion.32) | copy-start | bytes 3076
  421.3 20.5 %copy-start.94 = (f32[256]{0:T(256)}, f32[256]{0:T(256)S(1)}, u32[]{:S(2)}) copy-start(f32[256]{0:T(256)S(1)} %get-tuple-element.162) | copy-start | bytes 3076
  421.3 34.0 %copy-start.92 = (f32[256]{0:T(256)}, f32[256]{0:T(256)S(1)}, u32[]{:S(2)}) copy-start(f32[256]{0:T(256)S(1)} %get-tuple-element.163) | copy-start | bytes 3076
  421.9 19.9 %copy-start.98 = (f32[256]{0:T(256)}, f32[256]{0:T(256)S(1)}, u32[]{:S(2)}) copy-start(f32[256]{0:T(256)S(1)} %add_rsqrt_fusion.1) | copy-start | bytes 3076
  421.9 33.4 %copy-start.96 = (f32[256]{0:T(256)}, f32[256]{0:T(256)S(1)}, u32[]{:S(2)}) copy-start(f32[256]{0:T(256)S(1)} %add_rsqrt_fusion.3) | copy-start | bytes 3076
  421.9 41.9 %copy-start.107 = (f32[256]{0:T(256)}, f32[256]{0:T(256)S(1)}, u32[]{:S(2)}) copy-start(f32[256]{0:T(256)S(1)} %add_rsqrt_fusion.5) | copy-start | bytes 3076
  501.6 132.1 %copy-start.102 = (f32[16,256]{1,0:T(8,128)}, f32[16,256]{1,0:T(8,128)S(1)}, u32[]{:S(2)}) copy-start(f32[16,256]{1,0:T(8,128)S(1)} %get-tuple-element.142) | copy-start | bytes 49156
  541.9 18.0 %slice-start.4 = ((s8[10747904]{0:T(1024)(128)(4,1)}), s8[4194304]{0:T(1024)(128)(4,1)S(1)}, s32[]{:S(2)}) async-start(s8[10747904]{0:T(1024)(128)(4,1)} %bitcast.153), calls=%async_computation.15 | async-start | bytes 8388608
  593.9 288.4 %reduce-scatter.11.cloned.1.call-start = ((), (), s32[]{:S(2)}) async-start(), calls=%async_computation.10 | async-start | bytes 11354112 | tf_op jit(solution)/shard_map/reduce_scatter | solution.py:273
  614.9 428.3 %reduce-scatter.5.cloned.1.call-start = ((), (), s32[]{:S(2)}) async-start(), calls=%async_computation.7 | async-start | bytes 12976128 | tf_op jit(solution)/shard_map/reduce_scatter | solution.py:270
  682.8 597.0 %reduce-scatter.9.cloned.1.call-start = ((), (), s32[]{:S(2)}) async-start(), calls=%async_computation.9 | async-start | bytes 22167552 | tf_op jit(solution)/shard_map/reduce_scatter | solution.py:272
  (116 other events, 525.7 us)
Sparse Core Ops, SparseCore 0:
  10.9 109.4 all-gather.3
  123.2 306.0 all-gather.5
  432.2 66.1 all-gather.7
  594.0 110.1 reduce-scatter.6
  710.6 171.6 reduce-scatter.10
  888.8 154.3 reduce-scatter.4
  1046.2 233.6 reduce-scatter.8
